TPU v7x, 128 devices: a whole 4x4x4 slice. The times are simulated.
128 devices in a mesh: row: 16 (over y, x), col: 8 (over z, core).
Axes of the slice: x: 4, y: 4, z: 4, core: 2. Of those that a mesh axis runs over, the one named last changes fastest.
Arguments:
- features: bfloat16 [32768, 256], P(('row', 'col')), may hold values from -6 to 6
- out_degree: int32 [32768], P('row'), may hold values from 8 to 1024
- in_degree: int32 [32768], P('col'), may hold values from 8 to 1024
- tile_blocks: int32 [16, 8, 2, 128], P('row', 'col'), may hold values from 0 to 31, as said below
- tile_count: int32 [16, 8], P('row', 'col'), may hold values from 16 to 128, as said below
- tile_weights: bfloat16 [16, 8, 128, 128, 128], P('row', 'col'), may hold values from 0 to 4, as said below
- weight: bfloat16 [256, 256], replicated, may hold values from -0.375 to 0.375
- cotangent: bfloat16 [32768, 256], P(('col', 'row')), may hold values from -6 to 6
Outputs:
- hidden: bfloat16 [32768, 256], P(('col', 'row'))
- input_grad: bfloat16 [32768, 256], P(('row', 'col'))
- weight_grad: float32 [256, 256], replicated
Inputs may be any that keep to these rules, and one draw needn't show every extreme that they name: `tile_blocks`: entry [r, c, 0, s] is a target block below 32, entry [r, c, 1, s] a source block below 16; the pairs of one device position are distinct. `tile_count`: live tile slots of a device position are its first ones; some position has exactly 128. `tile_weights`: Non-negative edge weights.
All inputs are finite; a program needn't handle non-finite values.
Results may differ from a plain program's by a relative error of at most 0.0067.
Values may be sent and summed in bfloat16 or wider, within the bound.
No kernel may reach another device: no remote copies, remote signals or barrier semaphores. Data moves between devices by JAX's collectives and lax.ppermute only.
A program may use at most 192 MiB of HBM per device.

v0:
```python
import jax
import jax.numpy as jnp
from jax import lax
from jax.sharding import PartitionSpec as P

TILE = 128


def silu_slope(pre_act):
    gate_sig = jax.nn.sigmoid(pre_act)
    return gate_sig * (1.0 + pre_act * (1.0 - gate_sig))


def tile_sum(tile_vals, dst_ids, src_ids, live_count, inputs, dst_blocks, transpose):
    feat_width = inputs.shape[1]
    group_size = min(128, tile_vals.shape[0])
    block_stack = inputs.reshape(-1, TILE, feat_width)
    group_count = (live_count + group_size - 1) // group_size

    def add_group(group_at, running):
        first_slot = group_at * group_size
        picked = jnp.take(block_stack, src_ids, axis=0)
        if transpose:
            products = jnp.einsum(
                "trc,trh->tch", tile_vals, picked, preferred_element_type=jnp.float32
            )
        else:
            products = jnp.einsum(
                "trc,tch->trh", tile_vals, picked, preferred_element_type=jnp.float32
            )
        slot_ids = first_slot + jnp.arange(group_size)
        is_live = slot_ids < live_count
        masked = jnp.where(is_live[:, None], products.reshape(group_size, -1), 0.0)
        return running.at[dst_ids].add(masked)

    start_sum = jnp.zeros((dst_blocks, TILE * feat_width), jnp.float32)
    running = lax.fori_loop(0, group_count, add_group, start_sum)
    return running.reshape(dst_blocks * TILE, feat_width)


def shards(
    features, out_degree, in_degree, tile_blocks, tile_count, tile_weights, weight, cotangent
):
    row_count = features.shape[0]
    row_at = lax.axis_index("row")
    col_at = lax.axis_index("col")
    out_strip = lax.rsqrt(out_degree.astype(jnp.float32))
    in_strip = lax.rsqrt(in_degree.astype(jnp.float32))
    own_out = lax.dynamic_slice_in_dim(out_strip, col_at * row_count, row_count, 0)
    src_scaled = (features.astype(jnp.float32) * own_out[:, None]).astype(jnp.bfloat16)
    source = lax.all_gather(src_scaled, "col", axis=0, tiled=True)
    blocks = tile_blocks[0, 0]
    live_count = tile_count[0, 0]
    tile_vals = tile_weights[0, 0]
    partial_value = tile_sum(
        tile_vals, blocks[0], blocks[1], live_count, source, in_strip.shape[0] // TILE, False
    )
    contract_rows = (((0,), (0,)), ((), ()))
    summed = lax.psum(partial_value, "row")
    agg_strip = (summed * in_strip[:, None]).astype(jnp.bfloat16)
    pre_strip = jnp.dot(agg_strip, weight, preferred_element_type=jnp.float32)
    strip_grads = lax.all_gather(cotangent, "row", axis=0, tiled=True)
    grad_strip = (strip_grads.astype(jnp.float32) * silu_slope(pre_strip)).astype(jnp.bfloat16)
    own_pre = lax.dynamic_slice_in_dim(pre_strip, row_at * row_count, row_count, 0)
    hidden = jax.nn.silu(own_pre).astype(jnp.bfloat16)
    agg_rows = lax.dynamic_slice_in_dim(agg_strip, row_at * row_count, row_count, 0)
    pre_grad = lax.dynamic_slice_in_dim(grad_strip, row_at * row_count, row_count, 0)
    weight_part = lax.dot_general(
        agg_rows, pre_grad, contract_rows, preferred_element_type=jnp.float32
    )
    back_rows = jnp.dot(grad_strip, weight.T, preferred_element_type=jnp.float32)
    target_grad = (back_rows * in_strip[:, None]).astype(jnp.bfloat16)
    weight_grad = lax.psum(weight_part, ("row", "col"))
    back_part = tile_sum(
        tile_vals, blocks[1], blocks[0], live_count, target_grad, source.shape[0] // TILE, True
    )
    src_sum = lax.psum_scatter(back_part, "col", scatter_dimension=0, tiled=True)
    input_grad = (src_sum * own_out[:, None]).astype(jnp.bfloat16)
    return (hidden, input_grad, weight_grad)


def solution(mesh):
    placed = (
        P(("row", "col"), None),
        P("row"),
        P("col"),
        P("row", "col", None, None),
        P("row", "col"),
        P("row", "col", None, None, None),
        P(),
        P(("col", "row"), None),
    )
    return jax.shard_map(
        shards,
        mesh=mesh,
        in_specs=placed,
        out_specs=(P(("col", "row"), None), P(("row", "col"), None), P()),
        check_vma=False,
    )
```

profile of v0, /device:TPU:1, one launch (start us, length us, event | category | flops | bytes accessed | tf_op | source)
XLA Modules:
  0.0 580.1 jit_solution(587805703968408114)
XLA Ops:
  7.2 0.8 fusion.16
  8.5 1.7 multiply_convert_fusion.4
  10.9 0.8 slice_bitcast_fusion
  11.7 25.7 %all-gather.3.cloned.1.call-done = bf16[2048,256]{1,0:T(8,128)(2,1)} async-done(((bf16[256,256]{1,0:T(8,128)(2,1)}), bf16[2048,256]{1,0:T(8,128)(2,1)}) %all-gather.3.cloned.1.call-update) | async-done | bytes 1048592 | tf_op jit(solution)/shard_map/all_gather | solution.py:51
  37.4 2.3 broadcast_in_dim.54
  39.7 94.9 %while.20 = (s32[]{:T(128)}, f32[32,32768]{1,0:T(8,128)}, s32[]{:T(128)}, s32[128]{0:T(128)S(1)}, s32[]{:T(128)}, /*index=5*/s32[128]{0:T(128)S(1)}, bf16[16,128...) while((s32[]{:T(128)}, f32[32,32768]{1,0:T(8,128)}, s32[]{:T(128)}, ...), condition=%wide.region_2.3_spmd, body=%wide.region_0.2_spmd.sunk | while | flops 1086327552 | bytes 197141120 | solution.py:37
  39.8 6.6 %gather_fusion = bf16[128,128,256]{2,1,0:T(8,128)(2,1)} fusion(bf16[16,128,256]{2,1,0:T(8,128)(2,1)S(1)} %get-tuple-element.277, s32[1024]{0:T(1024)S(1)} %pad_clamp_fusion.4), kind=kCustom, calls=%fused_computation.clone.1 | custom fusion | bytes 16777728 | tf_op jit(solution)/shard_map/while/body/jit(_take)/gather | solution.py:22
  47.0 13.2 %convolution_bitcast_fusion.4 = f32[128,128,256]{1,2,0:T(8,128)} fusion(bf16[128,128,128]{2,1,0:T(8,128)(2,1)} %get-tuple-element.278, bf16[128,128,256]{2,1,0:T(8,128)(2,1)} %gather_fusion, pred[128]{0:T(512)(128)(4,1)S(1)} %get-tuple-element.237), kind=kOutput, calls=%fused_computation.5.clone.1 | convolution fusion | flops 1077936128 | bytes 29360256 | tf_op jit(solution)/shard_map/while/body/trc,tch->trh/dot_general | solution.py:28
  60.2 17.7 %copy.29 = f32[128,128,256]{0,2,1:T(8,128)} copy(f32[128,128,256]{1,2,0:T(8,128)} %convolution_bitcast_fusion.4) | data formatting | bytes 33554432 | tf_op jit(solution)/shard_map/while/body/trc,tch->trh/dot_general | solution.py:28
  77.9 11.2 %bitcast_select_fusion.4 = f32[128,32768]{0,1:T(8,128)} fusion(f32[128,128,256]{0,2,1:T(8,128)} %copy.29, pred[128]{0:T(512)(128)(4,1)S(1)} %get-tuple-element.238), kind=kLoop, calls=%fused_computation.4.clone.1 | loop fusion | flops 4194304 | bytes 33554560 | tf_op jit(solution)/shard_map/while/body/jit(_where)/select_n | solution.py:33
  89.1 17.4 %copy.30 = f32[128,32768]{1,0:T(8,128)} copy(f32[128,32768]{0,1:T(8,128)} %bitcast_select_fusion.4) | data formatting | bytes 33554432 | tf_op jit(solution)/shard_map/while/body/jit(_where)/select_n | solution.py:33
  106.6 27.7 %scatter_fusion = f32[32,32768]{1,0:T(8,128)} fusion(f32[32,32768]{1,0:T(8,128)} %get-tuple-element.262, s32[128]{0:T(128)S(1)} %get-tuple-element.235, f32[128,32768]{1,0:T(8,128)} %copy.30), kind=kCustom, calls=%fused_computation.2.clone.1 | custom fusion | flops 4194304 | bytes 50332160 | tf_op jit(solution)/shard_map/while/body/scatter-add | solution.py:34
  134.6 4.9 reshape.111
  140.4 101.8 %all-reduce.3.cloned.1.call-done = f32[4096,256]{1,0:T(8,128)} async-done(((f32[4096,256]{1,0:T(8,128)}), f32[4096,256]{1,0:T(8,128)}) %all-reduce.3.cloned.1.call-update) | async-done | bytes 4194320 | tf_op jit(solution)/shard_map/psum | solution.py:59
  242.2 2.6 multiply_convert_fusion.1
  244.7 42.9 %all-gather.5.cloned.1.call-done = bf16[4096,256]{1,0:T(8,128)(2,1)} async-done(((bf16[256,256]{1,0:T(8,128)(2,1)}), bf16[4096,256]{1,0:T(8,128)(2,1)}) %all-gather.5.cloned.1.call-update) | async-done | bytes 2097168 | tf_op jit(solution)/shard_map/all_gather | solution.py:62
  287.7 5.2 multiply_convert_fusion
  292.9 2.0 fusion.12
  295.0 92.8 %while.21 = (s32[]{:T(128)}, f32[16,32768]{1,0:T(8,128)S(1)}, s32[]{:T(128)}, s32[128]{0:T(128)S(1)}, s32[]{:T(128)}, /*index=5*/s32[128]{0:T(128)S(1)}, bf16[32...) while((s32[]{:T(128)}, f32[16,32768]{1,0:T(8,128)S(1)}, s32[]{:T(128)}, ...), condition=%wide.region_6.7_spmd, body=%wide.region_4.6_spmd.sunk | while | flops 1086327552 | bytes 197141120 | solution.py:37
  295.3 8.2 %gather_fusion.1 = bf16[128,128,256]{2,1,0:T(8,128)(2,1)} fusion(bf16[32,128,256]{2,1,0:T(8,128)(2,1)} %get-tuple-element.307, s32[1024]{0:T(1024)S(1)} %pad_clamp_fusion.5), kind=kCustom, calls=%fused_computation.1.clone.1 | custom fusion | bytes 16777728 | tf_op jit(solution)/shard_map/while/body/jit(_take)/gather | solution.py:22
  304.1 12.8 %convolution_bitcast_fusion.5 = f32[128,128,256]{1,2,0:T(8,128)} fusion(bf16[128,128,128]{2,1,0:T(8,128)(2,1)} %get-tuple-element.308, bf16[128,128,256]{2,1,0:T(8,128)(2,1)} %gather_fusion.1, pred[128]{0:T(512)(128)(4,1)S(1)} %get-tuple-element.249), kind=kOutput, calls=%fused_computation.19.clone.1 | convolution fusion | flops 1077936128 | bytes 29360256 | tf_op jit(solution)/shard_map/while/body/trc,trh->tch/dot_general | solution.py:24
  316.9 17.7 %copy.31 = f32[128,128,256]{0,2,1:T(8,128)} copy(f32[128,128,256]{1,2,0:T(8,128)} %convolution_bitcast_fusion.5) | data formatting | bytes 33554432 | tf_op jit(solution)/shard_map/while/body/trc,trh->tch/dot_general | solution.py:24
  334.6 11.3 %bitcast_select_fusion.5 = f32[128,32768]{0,1:T(8,128)} fusion(f32[128,128,256]{0,2,1:T(8,128)} %copy.31, pred[128]{0:T(512)(128)(4,1)S(1)} %get-tuple-element.250), kind=kLoop, calls=%fused_computation.18.clone.1 | loop fusion | flops 4194304 | bytes 33554560 | tf_op jit(solution)/shard_map/while/body/jit(_where)/select_n | solution.py:33
  345.9 17.4 %copy.32 = f32[128,32768]{1,0:T(8,128)} copy(f32[128,32768]{0,1:T(8,128)} %bitcast_select_fusion.5) | data formatting | bytes 33554432 | tf_op jit(solution)/shard_map/while/body/jit(_where)/select_n | solution.py:33
  363.3 24.3 %scatter_fusion.1 = f32[16,32768]{1,0:T(8,128)S(1)} fusion(f32[16,32768]{1,0:T(8,128)S(1)} %get-tuple-element.292, s32[128]{0:T(128)S(1)} %get-tuple-element.247, f32[128,32768]{1,0:T(8,128)} %copy.32), kind=kCustom, calls=%fused_computation.3.clone.1 | custom fusion | flops 4194304 | bytes 50332160 | tf_op jit(solution)/shard_map/while/body/scatter-add | solution.py:34
  387.9 1.5 reshape.113
  389.5 1.7 multiply_convert_fusion.3
  391.2 1.9 fusion.13
  393.1 28.5 %reduce-scatter.2.cloned.1.call-done = f32[256,256]{1,0:T(8,128)} async-done(((f32[2048,256]{1,0:T(8,128)}), f32[256,256]{1,0:T(8,128)}) %reduce-scatter.2.cloned.1.call-update) | async-done | bytes 262160 | tf_op jit(solution)/shard_map/reduce_scatter | solution.py:77
  421.5 1.7 multiply_convert_fusion.2
  423.3 148.3 %all-reduce.5.cloned.1.call-done = f32[256,256]{1,0:T(8,128)} async-done(((f32[256,256]{1,0:T(8,128)}), f32[256,256]{1,0:T(8,128)}) %all-reduce.5.cloned.1.call-update) | async-done | bytes 262160 | tf_op jit(solution)/shard_map/psum | solution.py:73
  571.6 1.7 copy.50
  (34 shorter events, 3.0 us)
Async XLA Ops:
  7.2 280.5 %copy-start = (bf16[256,256]{1,0:T(8,128)(2,1)S(1)}, bf16[256,256]{1,0:T(8,128)(2,1)}, u32[]{:S(2)}) copy-start(bf16[256,256]{1,0:T(8,128)(2,1)} %param.18) | copy-start | bytes 393220
  7.2 30.2 %all-gather.3.cloned.1.call-start = ((), (), s32[]{:S(2)}) async-start(), calls=%async_computation.1 | async-start | bytes 1179648 | tf_op jit(solution)/shard_map/all_gather | solution.py:51
  8.0 0.5 copy-start.6
  10.2 231.9 %all-reduce.3.cloned.1.call-start = ((), (), s32[]{:S(2)}) async-start(), calls=%async_computation.2 | async-start | bytes 8388608 | tf_op jit(solution)/shard_map/psum | solution.py:59
  37.4 2.3 copy-start.2
  139.5 0.8 copy-start.5
  139.5 148.1 %all-gather.5.cloned.1.call-start = ((), (), s32[]{:S(2)}) async-start(), calls=%async_computation.3 | async-start | bytes 2228224 | tf_op jit(solution)/shard_map/all_gather | solution.py:62
  140.3 281.3 %reduce-scatter.2.cloned.1.call-start = ((), (), s32[]{:S(2)}) async-start(), calls=%async_computation.4 | async-start | bytes 2359296 | tf_op jit(solution)/shard_map/reduce_scatter | solution.py:77
  244.7 48.1 %copy-start.3 = (bf16[4096,256]{1,0:T(8,128)(2,1)}, bf16[4096,256]{1,0:T(8,128)(2,1)S(1)}, u32[]{:S(2)}) copy-start(bf16[4096,256]{1,0:T(8,128)(2,1)S(1)} %multiply_convert_fusion.1) | copy-start | bytes 6291460
  292.9 2.0 copy-start.4
  387.9 33.7 %copy-start.7 = (f32[256]{0:T(256)S(1)}, f32[256]{0:T(256)}, u32[]{:S(2)}) copy-start(f32[256]{0:T(256)} %copy-done.6) | copy-start | bytes 3076
  387.9 185.4 %copy-start.1 = (bf16[256,256]{1,0:T(8,128)(2,1)S(1)}, bf16[256,256]{1,0:T(8,128)(2,1)}, u32[]{:S(2)}) copy-start(bf16[256,256]{1,0:T(8,128)(2,1)} %param.18) | copy-start | bytes 393220
  389.4 182.2 %all-reduce.5.cloned.1.call-start = ((), (), s32[]{:S(2)}) async-start(), calls=%async_computation.5 | async-start | bytes 524288 | tf_op jit(solution)/shard_map/psum | solution.py:73
Sparse Core Ops, SparseCore 0:
  10.3 27.0 all-gather.2
  139.7 102.4 all-reduce.2
  244.3 43.3 all-gather.4
  389.5 31.9 reduce-scatter.1
  426.7 144.8 all-reduce.4
where the time goes:
time: 582 us; the launch traced here: 580 us
  waiting for transfers between devices  348 us (60%)
  local copies, waits for them, and re-layouts  96.8 us (17%)
  other arithmetic  84.3 us (14%)
  matrix products  35.2 us (6%)
  between operations  14.8 us (3%)
    psum x1, waiting for transfers between devices, shards(): weight_grad = lax.psum(weight_part, ('row', 'col'))  148 us
    psum x1, waiting for transfers between devices, shards(): summed = lax.psum(partial_value, 'row')  102 us
    scatter-add x2, other arithmetic, add_group(): return running.at[dst_ids].add(masked)  52 us
    all_gather x1, waiting for transfers between devices, shards(): strip_grads = lax.all_gather(cotangent, 'row', axis=0, tiled=True)  42.9 us
    select_n x2, local copies, waits for them, and re-layouts, add_group(): masked = jnp.where(is_live[:, None], products.reshape(group_size, -1), 0.0)  34.9 us
    reduce_scatter x1, waiting for transfers between devices, shards(): lax.psum_scatter(back_part, 'col', scatter_dimension=0, tiled=True)  28.5 us
    all_gather x1, waiting for transfers between devices, shards(): source = lax.all_gather(src_scaled, 'col', axis=0, tiled=True)  25.7 us
    select_n x2, other arithmetic, add_group(): masked = jnp.where(is_live[:, None], products.reshape(group_size, -1), 0.0)  22.5 us
  transfers between devices with their start and end apart: 5, of which 5 were waited for; matrix products, arithmetic and copies ran while one was open for 1% of the time, Pallas kernels for 0%

commit v1 on v0

--- a/solution.py
+++ b/solution.py
@@ -59,7 +59,9 @@
     summed = lax.psum(partial_value, "row")
     agg_strip = (summed * in_strip[:, None]).astype(jnp.bfloat16)
     pre_strip = jnp.dot(agg_strip, weight, preferred_element_type=jnp.float32)
-    strip_grads = lax.all_gather(cotangent, "row", axis=0, tiled=True)
+    strip_grads = jnp.concatenate(
+        lax.all_to_all(jnp.stack([cotangent] * lax.axis_size("row")), "row", 0, 0), axis=0
+    )
     grad_strip = (strip_grads.astype(jnp.float32) * silu_slope(pre_strip)).astype(jnp.bfloat16)
     own_pre = lax.dynamic_slice_in_dim(pre_strip, row_at * row_count, row_count, 0)
     hidden = jax.nn.silu(own_pre).astype(jnp.bfloat16)

time: 582 us -> 564 us (0.969)
  waiting for transfers between devices: 348 us -> 320 us
  starting transfers between devices: 0.2 us -> 6.74 us
    all_gather x1 -> x0, waiting for transfers between devices: 42.9 us -> none  [shards(): strip_grads = lax.all_gather(cotangent, 'row', axis=0, tiled=True)]
    psum x1, waiting for transfers between devices: 102 us -> 118 us  [shards(): summed = lax.psum(partial_value, 'row')]
    all_to_all x0 -> x1, starting transfers between devices: none -> 6.58 us  [shards(): lax.all_to_all(jnp.stack([cotangent] * lax.axis_size('row')), 'row', 0, 0)]
  transfers between devices with their start and end apart: 5 -> 5, of which waited for: 5 -> 4; matrix products, arithmetic and copies ran while one was open for 1% -> 2% of each run, Pallas kernels for 0% -> 0%
where the time goes in v1:
time: 564 us; the launch traced here: 562 us
  waiting for transfers between devices  320 us (57%)
  local copies, waits for them, and re-layouts  99.2 us (18%)
  other arithmetic  84.3 us (15%)
  matrix products  36 us (6%)
  between operations  14.8 us (3%)
  starting transfers between devices  6.74 us (1%)
    psum x1, waiting for transfers between devices, shards(): weight_grad = lax.psum(weight_part, ('row', 'col'))  148 us
    psum x1, waiting for transfers between devices, shards(): summed = lax.psum(partial_value, 'row')  118 us
    scatter-add x2, other arithmetic, add_group(): return running.at[dst_ids].add(masked)  52 us
    select_n x2, local copies, waits for them, and re-layouts, add_group(): masked = jnp.where(is_live[:, None], products.reshape(group_size, -1), 0.0)  34.9 us
    reduce_scatter x1, waiting for transfers between devices, shards(): lax.psum_scatter(back_part, 'col', scatter_dimension=0, tiled=True)  27.6 us
    all_gather x1, waiting for transfers between devices, shards(): source = lax.all_gather(src_scaled, 'col', axis=0, tiled=True)  25.7 us
    select_n x2, other arithmetic, add_group(): masked = jnp.where(is_live[:, None], products.reshape(group_size, -1), 0.0)  22.5 us
    dot_general x1, local copies, waits for them, and re-layouts, add_group(): jnp.einsum('trc,tch->trh', tile_vals, picked, preferred_element_type=jnp....  17.7 us
  transfers between devices with their start and end apart: 5, of which 4 were waited for; matrix products, arithmetic and copies ran while one was open for 2% of the time, Pallas kernels for 0%

profile of v1, /device:TPU:1, one launch (start us, length us, event | category | flops | bytes accessed | tf_op | source)
XLA Modules:
  0.0 562.1 jit_solution(15400013099687349819)
XLA Ops:
  8.5 1.7 multiply_convert_fusion.3
  11.7 25.7 %all-gather.2.cloned.1.call-done = bf16[2048,256]{1,0:T(8,128)(2,1)} async-done(((bf16[256,256]{1,0:T(8,128)(2,1)}), bf16[2048,256]{1,0:T(8,128)(2,1)}) %all-gather.2.cloned.1.call-update) | async-done | bytes 1048592 | tf_op jit(solution)/shard_map/all_gather | solution.py:51
  37.4 2.3 broadcast_in_dim.54
  39.7 94.9 %while.20 = (s32[]{:T(128)}, f32[32,32768]{1,0:T(8,128)}, s32[]{:T(128)}, s32[128]{0:T(128)S(1)}, s32[]{:T(128)}, /*index=5*/s32[128]{0:T(128)S(1)}, bf16[16,128...) while((s32[]{:T(128)}, f32[32,32768]{1,0:T(8,128)}, s32[]{:T(128)}, ...), condition=%wide.region_2.3_spmd, body=%wide.region_0.2_spmd.sunk | while | flops 1086327552 | bytes 197141120 | solution.py:37
  39.8 6.6 %gather_fusion = bf16[128,128,256]{2,1,0:T(8,128)(2,1)} fusion(bf16[16,128,256]{2,1,0:T(8,128)(2,1)S(1)} %get-tuple-element.277, s32[1024]{0:T(1024)S(1)} %pad_clamp_fusion.4), kind=kCustom, calls=%fused_computation.clone.1 | custom fusion | bytes 16777728 | tf_op jit(solution)/shard_map/while/body/jit(_take)/gather | solution.py:22
  47.0 13.2 %convolution_bitcast_fusion.4 = f32[128,128,256]{1,2,0:T(8,128)} fusion(bf16[128,128,128]{2,1,0:T(8,128)(2,1)} %get-tuple-element.278, bf16[128,128,256]{2,1,0:T(8,128)(2,1)} %gather_fusion, pred[128]{0:T(512)(128)(4,1)S(1)} %get-tuple-element.237), kind=kOutput, calls=%fused_computation.5.clone.1 | convolution fusion | flops 1077936128 | bytes 29360256 | tf_op jit(solution)/shard_map/while/body/trc,tch->trh/dot_general | solution.py:28
  60.2 17.7 %copy.29 = f32[128,128,256]{0,2,1:T(8,128)} copy(f32[128,128,256]{1,2,0:T(8,128)} %convolution_bitcast_fusion.4) | data formatting | bytes 33554432 | tf_op jit(solution)/shard_map/while/body/trc,tch->trh/dot_general | solution.py:28
  77.9 11.2 %bitcast_select_fusion.4 = f32[128,32768]{0,1:T(8,128)} fusion(f32[128,128,256]{0,2,1:T(8,128)} %copy.29, pred[128]{0:T(512)(128)(4,1)S(1)} %get-tuple-element.238), kind=kLoop, calls=%fused_computation.4.clone.1 | loop fusion | flops 4194304 | bytes 33554560 | tf_op jit(solution)/shard_map/while/body/jit(_where)/select_n | solution.py:33
  89.1 17.4 %copy.30 = f32[128,32768]{1,0:T(8,128)} copy(f32[128,32768]{0,1:T(8,128)} %bitcast_select_fusion.4) | data formatting | bytes 33554432 | tf_op jit(solution)/shard_map/while/body/jit(_where)/select_n | solution.py:33
  106.6 27.7 %scatter_fusion = f32[32,32768]{1,0:T(8,128)} fusion(f32[32,32768]{1,0:T(8,128)} %get-tuple-element.262, s32[128]{0:T(128)S(1)} %get-tuple-element.235, f32[128,32768]{1,0:T(8,128)} %copy.30), kind=kCustom, calls=%fused_computation.2.clone.1 | custom fusion | flops 4194304 | bytes 50332160 | tf_op jit(solution)/shard_map/while/body/scatter-add | solution.py:34
  134.6 4.9 reshape.116
  139.5 0.9 copy-done.5
  140.4 1.5 stack.2
  142.0 6.6 %all-to-all-start = ((bf16[16,256,256]{2,1,0:T(8,128)(2,1)}), bf16[16,256,256]{2,1,0:T(8,128)(2,1)}, u32[]{:S(2)}, u32[]{:S(2)}) async-start(bf16[16,256,256]{2,1,0:T(8,128)(2,1)} %stack.2), calls=%async_computation | async-start | bytes 4194304 | tf_op jit(solution)/shard_map/all_to_all | solution.py:63
  148.6 118.4 %all-reduce.3.cloned.1.call-done = f32[4096,256]{1,0:T(8,128)} async-done(((f32[4096,256]{1,0:T(8,128)}), f32[4096,256]{1,0:T(8,128)}) %all-reduce.3.cloned.1.call-update) | async-done | bytes 4194320 | tf_op jit(solution)/shard_map/psum | solution.py:59
  267.1 2.6 multiply_convert_fusion
  269.7 6.0 %fusion.13 = (bf16[4096,256]{1,0:T(8,128)(2,1)S(1)}, f32[4096,256]{1,0:T(8,128)}) fusion(bf16[16,256,256]{2,1,0:T(8,128)(2,1)} %all-to-all-done, bf16[4096,256]{1,0:T(8,128)(2,1)S(1)} %multiply_convert_fusion, bf16[256,256]{1,0:T(8,128)(2,1)S(1)} %copy-done), kind=kOutput, calls=%fused_computation.35 | convolution fusion | flops 547356672 | bytes 10616832 | tf_op jit(solution)/shard_map/dot_general | solution.py:61
  275.7 2.0 fusion.12
  277.8 92.8 %while.21 = (s32[]{:T(128)}, f32[16,32768]{1,0:T(8,128)S(1)}, s32[]{:T(128)}, s32[128]{0:T(128)S(1)}, s32[]{:T(128)}, /*index=5*/s32[128]{0:T(128)S(1)}, bf16[32...) while((s32[]{:T(128)}, f32[16,32768]{1,0:T(8,128)S(1)}, s32[]{:T(128)}, ...), condition=%wide.region_6.7_spmd, body=%wide.region_4.6_spmd.sunk | while | flops 1086327552 | bytes 197141120 | solution.py:37
  278.1 8.2 %gather_fusion.1 = bf16[128,128,256]{2,1,0:T(8,128)(2,1)} fusion(bf16[32,128,256]{2,1,0:T(8,128)(2,1)} %get-tuple-element.307, s32[1024]{0:T(1024)S(1)} %pad_clamp_fusion.5), kind=kCustom, calls=%fused_computation.1.clone.1 | custom fusion | bytes 16777728 | tf_op jit(solution)/shard_map/while/body/jit(_take)/gather | solution.py:22
  286.9 12.8 %convolution_bitcast_fusion.5 = f32[128,128,256]{1,2,0:T(8,128)} fusion(bf16[128,128,128]{2,1,0:T(8,128)(2,1)} %get-tuple-element.308, bf16[128,128,256]{2,1,0:T(8,128)(2,1)} %gather_fusion.1, pred[128]{0:T(512)(128)(4,1)S(1)} %get-tuple-element.249), kind=kOutput, calls=%fused_computation.19.clone.1 | convolution fusion | flops 1077936128 | bytes 29360256 | tf_op jit(solution)/shard_map/while/body/trc,trh->tch/dot_general | solution.py:24
  299.7 17.7 %copy.31 = f32[128,128,256]{0,2,1:T(8,128)} copy(f32[128,128,256]{1,2,0:T(8,128)} %convolution_bitcast_fusion.5) | data formatting | bytes 33554432 | tf_op jit(solution)/shard_map/while/body/trc,trh->tch/dot_general | solution.py:24
  317.4 11.3 %bitcast_select_fusion.5 = f32[128,32768]{0,1:T(8,128)} fusion(f32[128,128,256]{0,2,1:T(8,128)} %copy.31, pred[128]{0:T(512)(128)(4,1)S(1)} %get-tuple-element.250), kind=kLoop, calls=%fused_computation.18.clone.1 | loop fusion | flops 4194304 | bytes 33554560 | tf_op jit(solution)/shard_map/while/body/jit(_where)/select_n | solution.py:33
  328.7 17.4 %copy.32 = f32[128,32768]{1,0:T(8,128)} copy(f32[128,32768]{0,1:T(8,128)} %bitcast_select_fusion.5) | data formatting | bytes 33554432 | tf_op jit(solution)/shard_map/while/body/jit(_where)/select_n | solution.py:33
  346.1 24.3 %scatter_fusion.1 = f32[16,32768]{1,0:T(8,128)S(1)} fusion(f32[16,32768]{1,0:T(8,128)S(1)} %get-tuple-element.292, s32[128]{0:T(128)S(1)} %get-tuple-element.247, f32[128,32768]{1,0:T(8,128)} %copy.32), kind=kCustom, calls=%fused_computation.3.clone.1 | custom fusion | flops 4194304 | bytes 50332160 | tf_op jit(solution)/shard_map/while/body/scatter-add | solution.py:34
  370.7 1.5 reshape.118
  372.3 1.7 multiply_convert_fusion.2
  374.0 1.9 fusion.14
  375.9 27.6 %reduce-scatter.2.cloned.1.call-done = f32[256,256]{1,0:T(8,128)} async-done(((f32[2048,256]{1,0:T(8,128)}), f32[256,256]{1,0:T(8,128)}) %reduce-scatter.2.cloned.1.call-update) | async-done | bytes 262160 | tf_op jit(solution)/shard_map/reduce_scatter | solution.py:79
  403.5 1.7 multiply_convert_fusion.1
  405.2 148.4 %all-reduce.5.cloned.1.call-done = f32[256,256]{1,0:T(8,128)} async-done(((f32[256,256]{1,0:T(8,128)}), f32[256,256]{1,0:T(8,128)}) %all-reduce.5.cloned.1.call-update) | async-done | bytes 262160 | tf_op jit(solution)/shard_map/psum | solution.py:75
  553.6 1.7 copy.50
  (36 shorter events, 3.8 us)
Async XLA Ops:
  7.2 262.5 %copy-start = (bf16[256,256]{1,0:T(8,128)(2,1)S(1)}, bf16[256,256]{1,0:T(8,128)(2,1)}, u32[]{:S(2)}) copy-start(bf16[256,256]{1,0:T(8,128)(2,1)} %param.18) | copy-start | bytes 393220
  7.2 30.2 %all-gather.2.cloned.1.call-start = ((), (), s32[]{:S(2)}) async-start(), calls=%async_computation.2 | async-start | bytes 1179648 | tf_op jit(solution)/shard_map/all_gather | solution.py:51
  8.0 0.5 copy-start.7
  10.2 256.8 %all-reduce.3.cloned.1.call-start = ((), (), s32[]{:S(2)}) async-start(), calls=%async_computation.3 | async-start | bytes 8388608 | tf_op jit(solution)/shard_map/psum | solution.py:59
  37.4 2.3 copy-start.2
  139.5 0.9 copy-start.5
  140.4 8.2 %copy-start.6 = (s32[4096]{0:T(1024)S(1)}, s32[4096]{0:T(1024)}, u32[]{:S(2)}) copy-start(s32[4096]{0:T(1024)} %param.14) | copy-start | bytes 49156
  142.0 127.7 %all-to-all-start = ((bf16[16,256,256]{2,1,0:T(8,128)(2,1)}), bf16[16,256,256]{2,1,0:T(8,128)(2,1)}, u32[]{:S(2)}, u32[]{:S(2)}) async-start(bf16[16,256,256]{2,1,0:T(8,128)(2,1)} %stack.2), calls=%async_computation | async-start | bytes 4194304 | tf_op jit(solution)/shard_map/all_to_all | solution.py:63
  148.5 254.9 %reduce-scatter.2.cloned.1.call-start = ((), (), s32[]{:S(2)}) async-start(), calls=%async_computation.4 | async-start | bytes 2359296 | tf_op jit(solution)/shard_map/reduce_scatter | solution.py:79
  269.7 6.0 %copy-start.3 = (bf16[4096,256]{1,0:T(8,128)(2,1)}, bf16[4096,256]{1,0:T(8,128)(2,1)S(1)}, u32[]{:S(2)}) copy-start(bf16[4096,256]{1,0:T(8,128)(2,1)S(1)} %multiply_convert_fusion) | copy-start | bytes 6291460
  275.7 2.0 copy-start.4
  370.7 32.8 %copy-start.8 = (f32[256]{0:T(256)S(1)}, f32[256]{0:T(256)}, u32[]{:S(2)}) copy-start(f32[256]{0:T(256)} %copy-done.7) | copy-start | bytes 3076
  370.7 184.6 %copy-start.1 = (bf16[256,256]{1,0:T(8,128)(2,1)S(1)}, bf16[256,256]{1,0:T(8,128)(2,1)}, u32[]{:S(2)}) copy-start(bf16[256,256]{1,0:T(8,128)(2,1)} %param.18) | copy-start | bytes 393220
  372.2 181.4 %all-reduce.5.cloned.1.call-start = ((), (), s32[]{:S(2)}) async-start(), calls=%async_computation.5 | async-start | bytes 524288 | tf_op jit(solution)/shard_map/psum | solution.py:75
Sparse Core Ops, SparseCore 0:
  10.3 27.0 all-gather.1
  139.7 127.3 all-reduce.2
  372.3 31.0 reduce-scatter.1
  408.6 144.8 all-reduce.4
